TPU v7x, 32 devices: a whole 2x2x4 slice. The times are simulated.
32 devices in a mesh: grp: 8 (over z, x), dev: 4 (over y, core).
Axes of the slice: x: 2, y: 2, z: 4, core: 2. Of those that a mesh axis runs over, the one named last changes fastest.
Arguments:
- block_states: float32 [256, 5, 4096], P(('grp', 'dev')), may hold values from -2 to 10.5, as said below
- dest_dev: int32 [256], P('grp'), may hold values from -1 to 3, as said below
- dest_slot: int32 [256], P('grp'), may hold values from 0 to 3, as said below
- neighbours: int32 [2, 128], P(None, 'grp'), may hold values from -1 to 15, as said below
- coarse_map: int32 [4, 32], P('dev'), may hold values from 0 to 31, each once within a row
Outputs:
- advanced: float32 [128, 5, 4096], P(('grp', 'dev'))
- registers: float32 [32, 5, 256], P(('grp', 'dev'))
Inputs may be any that keep to these rules, and one draw needn't show every extreme that they name: `block_states`: every slot holds a physical state: density 0.5 to 2, each velocity component -1 to 1, pressure 0.3 to 3. `dest_dev`: each pair of a receiving device index and a slot 0 .. 3 of a group gets exactly one patch; a device keeps its own patches or sends at most one patch to each of the next 3 device indices of its group (counted modulo 4) and to no other. `dest_slot`: see dest_dev. Index dev * 4 + slot within the group; neighbours are mutual (neighbours[1, a] = b exactly when neighbours[0, b] = a, within a group), a neighbour's index differs from the patch's own by at most 3, and -1 marks a domain boundary. `coarse_map`: for each device index a permutation: value m names register m // 4 in the group order, quadrant m % 4.
All inputs are finite; a program needn't handle non-finite values.
Results may differ from a plain program's by a relative error of at most 0.0003.
Values sent between devices are 32-bit elements; how exact they have to be, the bound alone decides.
No kernel may reach another device: no remote copies, remote signals or barrier semaphores. Data moves between devices by JAX's collectives and lax.ppermute only.
A program may use at most 64 MiB of HBM per device.

v0:
```python
import jax
import jax.numpy as jnp
from jax import lax
from jax.sharding import PartitionSpec as P

SIDE_LENGTH = 16
DEVICE_PATCHES = 4
P_DEV = 8
GAMMA = 1.4
COURANT = 0.2


def passed_along(block, axis, distance):
    devices = range(lax.axis_size(axis))
    route = [((i - distance) % len(devices), i) for i in devices]
    return lax.ppermute(block, axis, route)


def shifted(shard, axis, by):
    size = lax.axis_size(axis)
    pairs = [(i, i + by) for i in range(size) if 0 <= i + by < size]
    return lax.ppermute(shard, axis, pairs)


def primitives(conserved):
    density = conserved[..., 0, :, :]
    inverse = 1.0 / density
    vel_x = conserved[..., 1, :, :] * inverse
    vel_y = conserved[..., 2, :, :] * inverse
    vel_z = conserved[..., 3, :, :] * inverse
    kinetic = 0.5 * (
        conserved[..., 1, :, :] * vel_x
        + conserved[..., 2, :, :] * vel_y
        + conserved[..., 3, :, :] * vel_z
    )
    pressure = (GAMMA - 1.0) * (conserved[..., 4, :, :] - kinetic)
    return jnp.stack([density, vel_x, vel_y, vel_z, pressure], axis=-3)


def euler_flux(primitive):
    density = primitive[..., 0, :, :]
    vel_x = primitive[..., 1, :, :]
    vel_y = primitive[..., 2, :, :]
    vel_z = primitive[..., 3, :, :]
    pressure = primitive[..., 4, :, :]
    mass_flux = density * vel_x
    energy = pressure / (GAMMA - 1.0) + 0.5 * density * (
        vel_x * vel_x + vel_y * vel_y + vel_z * vel_z
    )
    fluxes = jnp.stack(
        [
            mass_flux,
            mass_flux * vel_x + pressure,
            mass_flux * vel_y,
            mass_flux * vel_z,
            vel_x * (energy + pressure),
        ],
        axis=-3,
    )
    conserved = jnp.stack([density, mass_flux, density * vel_y, density * vel_z, energy], axis=-3)
    speeds = jnp.abs(vel_x) + jnp.sqrt(GAMMA * pressure / density)
    return (fluxes, conserved, speeds)


def advance(block_volumes, lower_ghost, upper_ghost):
    extended = jnp.concatenate([lower_ghost, block_volumes, upper_ghost], axis=-2)
    primitive = primitives(extended)
    below_diff = primitive[..., 1:-1, :] - primitive[..., :-2, :]
    above_diff = primitive[..., 2:, :] - primitive[..., 1:-1, :]
    slopes = (
        0.5
        * (jnp.sign(below_diff) + jnp.sign(above_diff))
        * jnp.minimum(jnp.abs(below_diff), jnp.abs(above_diff))
    )
    centre = primitive[..., 1:-1, :]
    left_state = (centre + 0.5 * slopes)[..., :-1, :]
    right_state = (centre - 0.5 * slopes)[..., 1:, :]
    left_flux, left_cons, left_speed = euler_flux(left_state)
    right_flux, right_cons, right_speed = euler_flux(right_state)
    largest = jnp.maximum(left_speed, right_speed)[..., None, :, :]
    interface = 0.5 * (left_flux + right_flux) - 0.5 * largest * (right_cons - left_cons)
    updated = block_volumes - COURANT * (interface[..., 1:, :] - interface[..., :-1, :])
    return (updated, interface[..., -1, :])


def fill_edges(block_volumes, lower_ghost, upper_ghost, lower_nbr, upper_nbr):
    first = block_volumes[:, :, :1, :]
    last = block_volumes[:, :, -1:, :]
    lower_ghost = jnp.where(
        (lower_nbr < 0)[:, None, None, None], jnp.concatenate([first, first], axis=2), lower_ghost
    )
    upper_ghost = jnp.where(
        (upper_nbr < 0)[:, None, None, None], jnp.concatenate([last, last], axis=2), upper_ghost
    )
    return (lower_ghost, upper_ghost)


def coarsen(interface):
    half_edge = SIDE_LENGTH // 2
    shaped = interface.reshape(interface.shape[:-1] + (half_edge, 2, half_edge, 2))
    return shaped.mean(axis=(-3, -1))


def spread(coarse, quadrant):
    half_edge = SIDE_LENGTH // 2
    tiled = jnp.tile(coarse, (1,) * (coarse.ndim - 2) + (2, 2))
    row_ids = jnp.arange(SIDE_LENGTH, dtype=jnp.int32) // half_edge
    inside = (row_ids[:, None] == (quadrant // 2)[..., None, None]) & (
        row_ids[None, :] == (quadrant % 2)[..., None, None]
    )
    placed = tiled * inside.astype(tiled.dtype)[..., None, :, :]
    return placed.reshape(placed.shape[:-2] + (SIDE_LENGTH * SIDE_LENGTH,))


def selected_lines(weights, operand):
    flat = operand.reshape(operand.shape[0], -1)
    picked = jnp.dot(weights, flat, precision=lax.Precision.HIGHEST)
    return picked.reshape((weights.shape[0],) + operand.shape[1:])


def add_faces(totals, arrived, labels, lower_nbr, upper_nbr):
    below_sel = (lower_nbr[:, None] == labels[None, :]).astype(jnp.float32)
    above_sel = (upper_nbr[:, None] == labels[None, :]).astype(jnp.float32)
    return (
        totals[0] + selected_lines(below_sel, arrived[0]),
        totals[1] + selected_lines(above_sel, arrived[1]),
    )


def landing_rows(plan_dev, plan_slot, source_dev, my_dev, wanted):
    from_dev = lax.dynamic_index_in_dim(plan_dev, source_dev, 0, keepdims=False)
    from_slot = lax.dynamic_index_in_dim(plan_slot, source_dev, 0, keepdims=False)
    hits = (from_dev[None, :] == my_dev) & (from_slot[None, :] == wanted[:, None])
    return jnp.any(hits, axis=1).astype(jnp.float32)[:, None]


def local(block_states, dest_dev, dest_slot, neighbours, coarse_map):
    n_dev = lax.axis_size("dev")
    my_dev = lax.axis_index("dev")
    group_me = lax.axis_index("grp")
    cell_fields = block_states.shape[1]
    plane_cell_count = SIDE_LENGTH * SIDE_LENGTH
    wanted = jnp.arange(DEVICE_PATCHES, dtype=jnp.int32)
    mine_dev = lax.dynamic_slice_in_dim(dest_dev, my_dev * P_DEV, P_DEV)
    mine_slot = lax.dynamic_slice_in_dim(dest_slot, my_dev * P_DEV, P_DEV)
    retained_lines = (
        (mine_dev[None, :] == my_dev) & (mine_slot[None, :] == wanted[:, None])
    ).astype(jnp.float32)
    plan_dev = dest_dev.reshape(n_dev, P_DEV)
    plan_slot = dest_slot.reshape(n_dev, P_DEV)
    lower_all = neighbours[0]
    upper_all = neighbours[1]
    redistributed_blocks = selected_lines(retained_lines, block_states)
    for distance in range(1, DEVICE_PATCHES):
        target_dev = (my_dev + distance) % n_dev
        source_dev = (my_dev + n_dev - distance) % n_dev
        sending = (mine_dev == target_dev).astype(jnp.float32)[None, :]
        arrived = passed_along(selected_lines(sending, block_states), "dev", distance)
        redistributed_blocks = redistributed_blocks + selected_lines(
            landing_rows(plan_dev, plan_slot, source_dev, my_dev, wanted), arrived
        )
    block_volumes = redistributed_blocks.reshape(
        DEVICE_PATCHES, cell_fields, SIDE_LENGTH, plane_cell_count
    )
    lower_nbr = lax.dynamic_slice_in_dim(lower_all, my_dev * DEVICE_PATCHES, DEVICE_PATCHES)
    upper_nbr = lax.dynamic_slice_in_dim(upper_all, my_dev * DEVICE_PATCHES, DEVICE_PATCHES)
    top_layers = block_volumes[:, :, SIDE_LENGTH - 2 :, :]
    bottom_layers = block_volumes[:, :, :2, :]
    empty = jnp.zeros((DEVICE_PATCHES, cell_fields, 2, plane_cell_count), jnp.float32)
    ghosts = add_faces(
        (empty, empty),
        (top_layers, bottom_layers),
        my_dev * DEVICE_PATCHES + wanted,
        lower_nbr,
        upper_nbr,
    )
    from_below = shifted((top_layers, bottom_layers), "dev", 1)
    labels_below = jnp.where(my_dev > 0, (my_dev - 1) * DEVICE_PATCHES + wanted, -3)
    ghosts = add_faces(ghosts, from_below, labels_below, lower_nbr, upper_nbr)
    from_above = shifted((top_layers, bottom_layers), "dev", -1)
    labels_above = jnp.where(my_dev < n_dev - 1, (my_dev + 1) * DEVICE_PATCHES + wanted, -3)
    ghosts = add_faces(ghosts, from_above, labels_above, lower_nbr, upper_nbr)
    lower_ghost, upper_ghost = ghosts
    lower_ghost, upper_ghost = fill_edges(
        block_volumes, lower_ghost, upper_ghost, lower_nbr, upper_nbr
    )
    advanced, interface = advance(block_volumes, lower_ghost, upper_ghost)
    out_state = advanced.reshape(DEVICE_PATCHES, cell_fields, SIDE_LENGTH**3)
    column = coarse_map[0]
    half_edge = SIDE_LENGTH // 2
    coarse = coarsen(interface).reshape(DEVICE_PATCHES, cell_fields * half_edge * half_edge)
    arrived = lax.all_gather(coarse, "grp", axis=0, tiled=True)
    matched = (column // DEVICE_PATCHES == group_me).astype(jnp.float32)
    placed = spread(
        arrived.reshape(arrived.shape[0], cell_fields, half_edge, half_edge),
        column % DEVICE_PATCHES,
    )
    registers = jnp.einsum("k,kfc->fc", matched, placed, precision=lax.Precision.HIGHEST)[None]
    return (out_state, registers)


def solution(mesh):
    in_specs = (P(("grp", "dev"), None, None), P("grp"), P("grp"), P(None, "grp"), P("dev", None))
    out_specs = (P(("grp", "dev"), None, None), P(("grp", "dev"), None, None))
    return jax.shard_map(local, mesh=mesh, in_specs=in_specs, out_specs=out_specs, check_vma=False)
```

profile of v0, /device:TPU:0, one launch (start us, length us, event | category | flops | bytes accessed | tf_op | source)
XLA Modules:
  0.0 61.7 jit_solution(8667873022805380065)
XLA Ops:
  0.7 0.7 %copy-done.1 = s32[32]{0:T(128)S(1)} copy-done((s32[32]{0:T(128)S(1)}, s32[32]{0:T(128)}, u32[]{:S(2)}) %copy-start.1) | copy-done | bytes 152
  1.5 0.3 copy-done
  1.7 0.4 fusion.2
  2.2 2.5 %collective-permute-start.2 = (f32[1,5,4096]{2,1,0:T(8,128)S(1)}, f32[1,5,4096]{2,1,0:T(8,128)S(1)}, u32[]{:S(2)}, u32[]{:S(2)}) collective-permute-start(f32[1,5,4096]{2,1,0:T(8,128)S(1)} %copy.68), channel_id=1, source_target_pairs={{1,0},{2,1},{3,2},{0,3},{5,4},{6,5},{7,6},{4,7},{9,8},{10,9},{11,1... | collective-permute-start | bytes 245768 | tf_op jit(solution)/shard_map/ppermute | solution.py:16
  4.7 0.4 fusion.4
  5.2 0.7 %collective-permute-start.1 = (f32[1,5,4096]{2,1,0:T(8,128)S(1)}, f32[1,5,4096]{2,1,0:T(8,128)S(1)}, u32[]{:S(2)}, u32[]{:S(2)}) collective-permute-start(f32[1,5,4096]{2,1,0:T(8,128)S(1)} %copy.67), channel_id=1, source_target_pairs={{2,0},{3,1},{0,2},{1,3},{6,4},{7,5},{4,6},{5,7},{10,8},{11,9},{8,1... | collective-permute-start | bytes 245768 | tf_op jit(solution)/shard_map/ppermute | solution.py:16
  5.8 0.4 fusion.6
  6.3 0.3 collective-permute-start
  6.7 0.6 copy-done.4
  7.8 0.7 %copy-done.2 = s32[2,16]{1,0:T(2,128)S(1)} copy-done((s32[2,16]{1,0:T(2,128)S(1)}, s32[2,16]{1,0:T(2,128)}, u32[]{:S(2)}) %copy-start.2) | copy-done | bytes 152
  8.6 0.6 copy-done.3
  9.4 2.7 %collective-permute-done.1 = f32[1,5,4096]{2,1,0:T(8,128)S(1)} collective-permute-done((f32[1,5,4096]{2,1,0:T(8,128)S(1)}, f32[1,5,4096]{2,1,0:T(8,128)S(1)}, u32[]{:S(2)}, u32[]{:S(2)}) %collective-permute-start.1) | collective-permute-done | bytes 81952 | tf_op jit(solution)/shard_map/ppermute | solution.py:16
  12.1 0.4 collective-permute-done
  12.4 0.5 multiply_add_fusion
  12.9 0.2 reshape.339
  13.3 1.3 %collective-permute-start.5 = (f32[4,5,2,256]{3,2,1,0:T(2,128)S(1)}, f32[4,5,2,256]{3,2,1,0:T(2,128)S(1)}, u32[]{:S(2)}, u32[]{:S(2)}) collective-permute-start(f32[4,5,2,256]{3,2,1,0:T(2,128)S(1)} %copy.77), channel_id=1, source_target_pairs={{0,1},{1,2},{2,3},{4,5},{5,6},{6,7},{8,9},{9,10},{10,11},{12,13},{... | collective-permute-start | bytes 122888 | tf_op jit(solution)/shard_map/ppermute | solution.py:22
  14.6 1.3 %collective-permute-start.6 = (f32[4,5,2,256]{3,2,1,0:T(2,128)S(1)}, f32[4,5,2,256]{3,2,1,0:T(2,128)S(1)}, u32[]{:S(2)}, u32[]{:S(2)}) collective-permute-start(f32[4,5,2,256]{3,2,1,0:T(2,128)S(1)} %copy.77), channel_id=1, source_target_pairs={{1,0},{2,1},{3,2},{5,4},{6,5},{7,6},{9,8},{10,9},{11,10},{13,12},{... | collective-permute-start | bytes 122888 | tf_op jit(solution)/shard_map/ppermute | solution.py:22
  15.9 4.7 %collective-permute-start.3 = (f32[4,5,2,256]{3,2,1,0:T(2,128)S(1)}, f32[4,5,2,256]{3,2,1,0:T(2,128)S(1)}, u32[]{:S(2)}, u32[]{:S(2)}) collective-permute-start(f32[4,5,2,256]{3,2,1,0:T(2,128)S(1)} %copy.76), channel_id=1, source_target_pairs={{0,1},{1,2},{2,3},{4,5},{5,6},{6,7},{8,9},{9,10},{10,11},{12,13},{... | collective-permute-start | bytes 122888 | tf_op jit(solution)/shard_map/ppermute | solution.py:22
  20.7 1.3 %collective-permute-start.4 = (f32[4,5,2,256]{3,2,1,0:T(2,128)S(1)}, f32[4,5,2,256]{3,2,1,0:T(2,128)S(1)}, u32[]{:S(2)}, u32[]{:S(2)}) collective-permute-start(f32[4,5,2,256]{3,2,1,0:T(2,128)S(1)} %copy.76), channel_id=1, source_target_pairs={{1,0},{2,1},{3,2},{5,4},{6,5},{7,6},{9,8},{10,9},{11,10},{13,12},{... | collective-permute-start | bytes 122888 | tf_op jit(solution)/shard_map/ppermute | solution.py:22
  22.5 0.2 convolution_add_fusion.1
  22.8 0.2 fusion
  23.1 0.2 convolution_add_fusion.3
  23.3 1.7 %collective-permute-done.4 = f32[4,5,2,256]{3,2,1,0:T(2,128)S(1)} collective-permute-done((f32[4,5,2,256]{3,2,1,0:T(2,128)S(1)}, f32[4,5,2,256]{3,2,1,0:T(2,128)S(1)}, u32[]{:S(2)}, u32[]{:S(2)}) %collective-permute-start.4) | collective-permute-done | bytes 40992 | tf_op jit(solution)/shard_map/ppermute | solution.py:22
  25.1 0.2 fusion.1
  25.7 0.4 slice_add_fusion
  27.1 0.8 %fusion.11 = f32[4,5,16,256]{3,0,2,1:T(4,128)} fusion(f32[4,5,16,256]{3,0,2,1:T(4,128)S(1)} %bitcast.134, f32[4,5,17,256]{3,0,2,1:T(4,128)S(1)} %multiply_subtract_fusion), kind=kLoop, calls=%fused_computation.21 | loop fusion | flops 245760 | bytes 1310720 | tf_op jit(solution)/shard_map/sub | solution.py:82
  28.2 0.4 reduce_sum.9
  28.6 0.3 copy.64
  29.0 31.1 %all-gather = f32[8,4,320]{2,1,0:T(4,128)S(1)} all-gather(f32[1,4,320]{2,1,0:T(4,128)S(1)} %reshape.347), channel_id=1, replica_groups=mesh['grp'=8,'dev'=4] {'grp'}, dimensions={0}, use_global_device_ids=true | all-gather | bytes 46080 | tf_op jit(solution)/shard_map/all_gather | solution.py:192
  60.1 0.2 tile.8
  60.7 0.4 fusion.27
  61.1 0.6 %broadcast_in_dim.19 = f32[1,5,256]{2,0,1:T(1,128)} reshape(f32[5,256]{1,0:T(8,128)S(1)} %bitcast.147) | data formatting | bytes 10240 | tf_op jit(solution)/shard_map/broadcast_in_dim | solution.py:198
  (76 shorter events, 3.8 us)
Async XLA Ops:
  0.6 1.1 %copy-start = (f32[8,5,4096]{2,0,1:T(8,128)S(1)}, f32[8,5,4096]{2,0,1:T(8,128)}, u32[]{:S(2)}) copy-start(f32[8,5,4096]{2,0,1:T(8,128)} %param.5) | copy-start | bytes 1966084
  0.7 0.7 %copy-start.1 = (s32[32]{0:T(128)S(1)}, s32[32]{0:T(128)}, u32[]{:S(2)}) copy-start(s32[32]{0:T(128)} %param.6) | copy-start | bytes 388
  2.2 7.1 %collective-permute-start.2 = (f32[1,5,4096]{2,1,0:T(8,128)S(1)}, f32[1,5,4096]{2,1,0:T(8,128)S(1)}, u32[]{:S(2)}, u32[]{:S(2)}) collective-permute-start(f32[1,5,4096]{2,1,0:T(8,128)S(1)} %copy.68), channel_id=1, source_target_pairs={{1,0},{2,1},{3,2},{0,3},{5,4},{6,5},{7,6},{4,7},{9,8},{10,9},{11,1... | collective-permute-start | bytes 245768 | tf_op jit(solution)/shard_map/ppermute | solution.py:16
  5.2 6.9 %collective-permute-start.1 = (f32[1,5,4096]{2,1,0:T(8,128)S(1)}, f32[1,5,4096]{2,1,0:T(8,128)S(1)}, u32[]{:S(2)}, u32[]{:S(2)}) collective-permute-start(f32[1,5,4096]{2,1,0:T(8,128)S(1)} %copy.67), channel_id=1, source_target_pairs={{2,0},{3,1},{0,2},{1,3},{6,4},{7,5},{4,6},{5,7},{10,8},{11,9},{8,1... | collective-permute-start | bytes 245768 | tf_op jit(solution)/shard_map/ppermute | solution.py:16
  6.3 6.1 %collective-permute-start = (f32[1,5,4096]{2,1,0:T(8,128)S(1)}, f32[1,5,4096]{2,1,0:T(8,128)S(1)}, u32[]{:S(2)}, u32[]{:S(2)}) collective-permute-start(f32[1,5,4096]{2,1,0:T(8,128)S(1)} %copy.66), channel_id=1, source_target_pairs={{3,0},{0,1},{1,2},{2,3},{7,4},{4,5},{5,6},{6,7},{11,8},{8,9},{9,10... | collective-permute-start | bytes 245768 | tf_op jit(solution)/shard_map/ppermute | solution.py:16
  6.6 0.7 %copy-start.4 = (s32[32]{0:T(128)S(1)}, s32[32]{0:T(128)}, u32[]{:S(2)}) copy-start(s32[32]{0:T(128)} %param.7) | copy-start | bytes 388
  7.8 0.7 %copy-start.2 = (s32[2,16]{1,0:T(2,128)S(1)}, s32[2,16]{1,0:T(2,128)}, u32[]{:S(2)}) copy-start(s32[2,16]{1,0:T(2,128)} %param.8) | copy-start | bytes 388
  8.5 0.7 %copy-start.3 = (s32[1,32]{1,0:T(1,128)S(1)}, s32[1,32]{1,0:T(1,128)}, u32[]{:S(2)}) copy-start(s32[1,32]{1,0:T(1,128)} %param.9) | copy-start | bytes 388
  13.3 9.2 %collective-permute-start.5 = (f32[4,5,2,256]{3,2,1,0:T(2,128)S(1)}, f32[4,5,2,256]{3,2,1,0:T(2,128)S(1)}, u32[]{:S(2)}, u32[]{:S(2)}) collective-permute-start(f32[4,5,2,256]{3,2,1,0:T(2,128)S(1)} %copy.77), channel_id=1, source_target_pairs={{0,1},{1,2},{2,3},{4,5},{5,6},{6,7},{8,9},{9,10},{10,11},{12,13},{... | collective-permute-start | bytes 122888 | tf_op jit(solution)/shard_map/ppermute | solution.py:22
  14.6 8.2 %collective-permute-start.6 = (f32[4,5,2,256]{3,2,1,0:T(2,128)S(1)}, f32[4,5,2,256]{3,2,1,0:T(2,128)S(1)}, u32[]{:S(2)}, u32[]{:S(2)}) collective-permute-start(f32[4,5,2,256]{3,2,1,0:T(2,128)S(1)} %copy.77), channel_id=1, source_target_pairs={{1,0},{2,1},{3,2},{5,4},{6,5},{7,6},{9,8},{10,9},{11,10},{13,12},{... | collective-permute-start | bytes 122888 | tf_op jit(solution)/shard_map/ppermute | solution.py:22
  15.9 7.1 %collective-permute-start.3 = (f32[4,5,2,256]{3,2,1,0:T(2,128)S(1)}, f32[4,5,2,256]{3,2,1,0:T(2,128)S(1)}, u32[]{:S(2)}, u32[]{:S(2)}) collective-permute-start(f32[4,5,2,256]{3,2,1,0:T(2,128)S(1)} %copy.76), channel_id=1, source_target_pairs={{0,1},{1,2},{2,3},{4,5},{5,6},{6,7},{8,9},{9,10},{10,11},{12,13},{... | collective-permute-start | bytes 122888 | tf_op jit(solution)/shard_map/ppermute | solution.py:22
  20.7 4.4 %collective-permute-start.4 = (f32[4,5,2,256]{3,2,1,0:T(2,128)S(1)}, f32[4,5,2,256]{3,2,1,0:T(2,128)S(1)}, u32[]{:S(2)}, u32[]{:S(2)}) collective-permute-start(f32[4,5,2,256]{3,2,1,0:T(2,128)S(1)} %copy.76), channel_id=1, source_target_pairs={{1,0},{2,1},{3,2},{5,4},{6,5},{7,6},{9,8},{10,9},{11,10},{13,12},{... | collective-permute-start | bytes 122888 | tf_op jit(solution)/shard_map/ppermute | solution.py:22
where the time goes:
time: 62 us; the launch traced here: 61.7 us
  blocking collectives  31.1 us (50%)
  starting transfers between devices  12 us (19%)
  local copies, waits for them, and re-layouts  5.52 us (9%)
  waiting for transfers between devices  4.78 us (8%)
  other arithmetic  3.65 us (6%)
  matrix products  3.52 us (6%)
  between operations  1.14 us (2%)
    all_gather x1, blocking collectives, local(): arrived = lax.all_gather(coarse, 'grp', axis=0, tiled=True)  31.1 us
    ppermute x4, starting transfers between devices, shifted(): return lax.ppermute(shard, axis, pairs)  8.6 us
    ppermute x3, starting transfers between devices, passed_along(): return lax.ppermute(block, axis, route)  3.39 us
    dot_general x10, matrix products, selected_lines(): picked = jnp.dot(weights, flat, precision=lax.Precision.HIGHEST)  3.09 us
    ppermute x3, waiting for transfers between devices, passed_along(): return lax.ppermute(block, axis, route)  3.08 us
    unnamed x16, local copies, waits for them, and re-layouts  2.97 us
    ppermute x4, waiting for transfers between devices, shifted(): return lax.ppermute(shard, axis, pairs)  1.69 us
  transfers between devices with their start and end apart: 7, of which 3 were waited for; matrix products, arithmetic and copies ran while one was open for 5% of the time, Pallas kernels for 0%

commit v1 on v0

--- a/solution.py
+++ b/solution.py
@@ -189,7 +189,22 @@
     column = coarse_map[0]
     half_edge = SIDE_LENGTH // 2
     coarse = coarsen(interface).reshape(DEVICE_PATCHES, cell_fields * half_edge * half_edge)
-    arrived = lax.all_gather(coarse, "grp", axis=0, tiled=True)
+    ways, here, step = (lax.axis_size("grp"), lax.axis_index("grp"), coarse.shape[0])
+    shape = [n * ways if d == 0 else n for d, n in enumerate(coarse.shape)]
+    arrived = lax.dynamic_update_slice_in_dim(
+        jnp.zeros(shape, coarse.dtype), coarse, here * step, axis=0
+    )
+    going_up = going_down = coarse
+    for far in range(1, ways // 2 + 1):
+        going_up = lax.ppermute(going_up, "grp", [(d, (d + 1) % ways) for d in range(ways)])
+        arrived = lax.dynamic_update_slice_in_dim(
+            arrived, going_up, (here - far) % ways * step, axis=0
+        )
+        if 2 * far < ways:
+            going_down = lax.ppermute(going_down, "grp", [(d, (d - 1) % ways) for d in range(ways)])
+            arrived = lax.dynamic_update_slice_in_dim(
+                arrived, going_down, (here + far) % ways * step, axis=0
+            )
     matched = (column // DEVICE_PATCHES == group_me).astype(jnp.float32)
     placed = spread(
         arrived.reshape(arrived.shape[0], cell_fields, half_edge, half_edge),

time: 62 us -> 58.7 us (0.947)
  blocking collectives: 31.1 us -> 0 us
  starting transfers between devices: 12 us -> 26.4 us
  local copies, waits for them, and re-layouts: 5.52 us -> 14.2 us
  waiting for transfers between devices: 4.78 us -> 9.42 us
    all_gather x1 -> x0, blocking collectives: 31.1 us -> none  [local(): arrived = lax.all_gather(coarse, 'grp', axis=0, tiled=True)]
    ppermute x0 -> x7, starting transfers between devices: none -> 14.4 us  [the longest x3 12.8 us: local(): lax.ppermute(going_down, 'grp', [(d, (d - 1) % ways) for d in range(ways)])]
    dynamic_update_slice x0 -> x8, local copies, waits for them, and re-layouts: none -> 8.05 us  [the longest x4 4.17 us: local(): lax.dynamic_update_slice_in_dim(arrived, going_up, (here - far) % ways *...]
    ppermute x0 -> x7, waiting for transfers between devices: none -> 4.54 us  [the longest x4 4.53 us: local(): lax.ppermute(going_up, 'grp', [(d, (d + 1) % ways) for d in range(ways)])]
    ppermute x0 -> x7, local copies, waits for them, and re-layouts: none -> 0.95 us  [the longest x4 0.55 us: local(): lax.ppermute(going_up, 'grp', [(d, (d + 1) % ways) for d in range(ways)])]
    unnamed x16 -> x15, local copies, waits for them, and re-layouts: 2.97 us -> 2.88 us
  transfers between devices with their start and end apart: 7 -> 14, of which waited for: 3 -> 6; matrix products, arithmetic and copies ran while one was open for 5% -> 20% of each run, Pallas kernels for 0% -> 0%
where the time goes in v1:
time: 58.7 us; the launch traced here: 58.5 us
  starting transfers between devices  26.4 us (45%)
  local copies, waits for them, and re-layouts  14.2 us (24%)
  waiting for transfers between devices  9.42 us (16%)
  other arithmetic  3.63 us (6%)
  matrix products  3.52 us (6%)
  between operations  1.32 us (2%)
    ppermute x3, starting transfers between devices, local(): lax.ppermute(going_down, 'grp', [(d, (d - 1) % ways) for d in range(ways)])  12.8 us
    ppermute x4, starting transfers between devices, shifted(): return lax.ppermute(shard, axis, pairs)  8.6 us
    ppermute x4, waiting for transfers between devices, local(): lax.ppermute(going_up, 'grp', [(d, (d + 1) % ways) for d in range(ways)])  4.53 us
    dynamic_update_slice x4, local copies, waits for them, and re-layouts, local(): lax.dynamic_update_slice_in_dim(arrived, going_up, (here - far) % ways *...  4.17 us
    ppermute x3, starting transfers between devices, passed_along(): return lax.ppermute(block, axis, route)  3.39 us
    ppermute x3, waiting for transfers between devices, passed_along(): return lax.ppermute(block, axis, route)  3.19 us
    dynamic_update_slice x3, local copies, waits for them, and re-layouts, local(): lax.dynamic_update_slice_in_dim(arrived, going_down, (here + far) % ways...  3.12 us
    dot_general x10, matrix products, selected_lines(): picked = jnp.dot(weights, flat, precision=lax.Precision.HIGHEST)  3.09 us
  transfers between devices with their start and end apart: 14, of which 6 were waited for; matrix products, arithmetic and copies ran while one was open for 20% of the time, Pallas kernels for 0%

profile of v1, /device:TPU:0, one launch (start us, length us, event | category | flops | bytes accessed | tf_op | source)
XLA Modules:
  0.0 58.5 jit_solution(16362177235141520963)
XLA Ops:
  0.7 0.7 %copy-done.1 = s32[32]{0:T(128)S(1)} copy-done((s32[32]{0:T(128)S(1)}, s32[32]{0:T(128)}, u32[]{:S(2)}) %copy-start.1) | copy-done | bytes 152
  2.2 2.5 %collective-permute-start.2 = (f32[1,5,4096]{2,1,0:T(8,128)S(1)}, f32[1,5,4096]{2,1,0:T(8,128)S(1)}, u32[]{:S(2)}, u32[]{:S(2)}) collective-permute-start(f32[1,5,4096]{2,1,0:T(8,128)S(1)} %copy.86), channel_id=1, source_target_pairs={{1,0},{2,1},{3,2},{0,3},{5,4},{6,5},{7,6},{4,7},{9,8},{10,9},{11,1... | collective-permute-start | bytes 245768 | tf_op jit(solution)/shard_map/ppermute | solution.py:16
  5.2 0.7 %collective-permute-start.1 = (f32[1,5,4096]{2,1,0:T(8,128)S(1)}, f32[1,5,4096]{2,1,0:T(8,128)S(1)}, u32[]{:S(2)}, u32[]{:S(2)}) collective-permute-start(f32[1,5,4096]{2,1,0:T(8,128)S(1)} %copy.85), channel_id=1, source_target_pairs={{2,0},{3,1},{0,2},{1,3},{6,4},{7,5},{4,6},{5,7},{10,8},{11,9},{8,1... | collective-permute-start | bytes 245768 | tf_op jit(solution)/shard_map/ppermute | solution.py:16
  6.7 0.6 copy-done.4
  7.8 0.7 %copy-done.2 = s32[2,16]{1,0:T(2,128)S(1)} copy-done((s32[2,16]{1,0:T(2,128)S(1)}, s32[2,16]{1,0:T(2,128)}, u32[]{:S(2)}) %copy-start.2) | copy-done | bytes 152
  8.6 0.6 copy-done.3
  9.2 2.8 %collective-permute-done.1 = f32[1,5,4096]{2,1,0:T(8,128)S(1)} collective-permute-done((f32[1,5,4096]{2,1,0:T(8,128)S(1)}, f32[1,5,4096]{2,1,0:T(8,128)S(1)}, u32[]{:S(2)}, u32[]{:S(2)}) %collective-permute-start.1) | collective-permute-done | bytes 81952 | tf_op jit(solution)/shard_map/ppermute | solution.py:16
  12.4 0.5 multiply_add_fusion
  13.3 1.3 %collective-permute-start.5 = (f32[4,5,2,256]{3,2,1,0:T(2,128)S(1)}, f32[4,5,2,256]{3,2,1,0:T(2,128)S(1)}, u32[]{:S(2)}, u32[]{:S(2)}) collective-permute-start(f32[4,5,2,256]{3,2,1,0:T(2,128)S(1)} %copy.95), channel_id=1, source_target_pairs={{0,1},{1,2},{2,3},{4,5},{5,6},{6,7},{8,9},{9,10},{10,11},{12,13},{... | collective-permute-start | bytes 122888 | tf_op jit(solution)/shard_map/ppermute | solution.py:22
  14.6 1.3 %collective-permute-start.6 = (f32[4,5,2,256]{3,2,1,0:T(2,128)S(1)}, f32[4,5,2,256]{3,2,1,0:T(2,128)S(1)}, u32[]{:S(2)}, u32[]{:S(2)}) collective-permute-start(f32[4,5,2,256]{3,2,1,0:T(2,128)S(1)} %copy.95), channel_id=1, source_target_pairs={{1,0},{2,1},{3,2},{5,4},{6,5},{7,6},{9,8},{10,9},{11,10},{13,12},{... | collective-permute-start | bytes 122888 | tf_op jit(solution)/shard_map/ppermute | solution.py:22
  15.9 4.7 %collective-permute-start.3 = (f32[4,5,2,256]{3,2,1,0:T(2,128)S(1)}, f32[4,5,2,256]{3,2,1,0:T(2,128)S(1)}, u32[]{:S(2)}, u32[]{:S(2)}) collective-permute-start(f32[4,5,2,256]{3,2,1,0:T(2,128)S(1)} %copy.94), channel_id=1, source_target_pairs={{0,1},{1,2},{2,3},{4,5},{5,6},{6,7},{8,9},{9,10},{10,11},{12,13},{... | collective-permute-start | bytes 122888 | tf_op jit(solution)/shard_map/ppermute | solution.py:22
  20.7 1.3 %collective-permute-start.4 = (f32[4,5,2,256]{3,2,1,0:T(2,128)S(1)}, f32[4,5,2,256]{3,2,1,0:T(2,128)S(1)}, u32[]{:S(2)}, u32[]{:S(2)}) collective-permute-start(f32[4,5,2,256]{3,2,1,0:T(2,128)S(1)} %copy.94), channel_id=1, source_target_pairs={{1,0},{2,1},{3,2},{5,4},{6,5},{7,6},{9,8},{10,9},{11,10},{13,12},{... | collective-permute-start | bytes 122888 | tf_op jit(solution)/shard_map/ppermute | solution.py:22
  23.3 1.7 %collective-permute-done.4 = f32[4,5,2,256]{3,2,1,0:T(2,128)S(1)} collective-permute-done((f32[4,5,2,256]{3,2,1,0:T(2,128)S(1)}, f32[4,5,2,256]{3,2,1,0:T(2,128)S(1)}, u32[]{:S(2)}, u32[]{:S(2)}) %collective-permute-start.4) | collective-permute-done | bytes 40992 | tf_op jit(solution)/shard_map/ppermute | solution.py:22
  27.3 0.4 reduce_sum.9
  28.1 1.5 %collective-permute-start.7 = (f32[4,320]{1,0:T(4,128)S(1)}, f32[4,320]{1,0:T(4,128)S(1)}, u32[]{:S(2)}, u32[]{:S(2)}) collective-permute-start(f32[4,320]{1,0:T(4,128)S(1)} %div.74), channel_id=1, source_target_pairs={{0,4},{4,8},{8,12},{12,16},{16,20},{20,24},{24,28},{28,0},{1,5},{5... | collective-permute-start | bytes 15368 | tf_op jit(solution)/shard_map/ppermute | solution.py:199
  29.8 3.2 %collective-permute-start.8 = (f32[4,320]{1,0:T(4,128)S(1)}, f32[4,320]{1,0:T(4,128)S(1)}, u32[]{:S(2)}, u32[]{:S(2)}) collective-permute-start(f32[4,320]{1,0:T(4,128)S(1)} %div.74), channel_id=1, source_target_pairs={{0,28},{4,0},{8,4},{12,8},{16,12},{20,16},{24,20},{28,24},{1,29},{... | collective-permute-start | bytes 15368 | tf_op jit(solution)/shard_map/ppermute | solution.py:204
  33.0 1.5 %collective-permute-done.7 = f32[4,320]{1,0:T(4,128)S(1)} collective-permute-done((f32[4,320]{1,0:T(4,128)S(1)}, f32[4,320]{1,0:T(4,128)S(1)}, u32[]{:S(2)}, u32[]{:S(2)}) %collective-permute-start.7) | collective-permute-done | bytes 5152 | tf_op jit(solution)/shard_map/ppermute | solution.py:199
  34.6 4.8 %collective-permute-start.10 = (f32[4,320]{1,0:T(4,128)S(1)}, f32[4,320]{1,0:T(4,128)S(1)}, u32[]{:S(2)}, u32[]{:S(2)}) collective-permute-start(f32[4,320]{1,0:T(4,128)S(1)} %collective-permute-done.8), channel_id=1, source_target_pairs={{0,28},{4,0},{8,4},{12,8},{16,12},{20,16},{24,20},{28,24},{1,29},{... | collective-permute-start | bytes 15368 | tf_op jit(solution)/shard_map/ppermute | solution.py:204
  39.4 1.5 %collective-permute-done.9 = f32[4,320]{1,0:T(4,128)S(1)} collective-permute-done((f32[4,320]{1,0:T(4,128)S(1)}, f32[4,320]{1,0:T(4,128)S(1)}, u32[]{:S(2)}, u32[]{:S(2)}) %collective-permute-start.9) | collective-permute-done | bytes 5152 | tf_op jit(solution)/shard_map/ppermute | solution.py:199
  40.9 4.8 %collective-permute-start.12 = (f32[4,320]{1,0:T(4,128)S(1)}, f32[4,320]{1,0:T(4,128)S(1)}, u32[]{:S(2)}, u32[]{:S(2)}) collective-permute-start(f32[4,320]{1,0:T(4,128)S(1)} %collective-permute-done.10), channel_id=1, source_target_pairs={{0,28},{4,0},{8,4},{12,8},{16,12},{20,16},{24,20},{28,24},{1,29},{... | collective-permute-start | bytes 15368 | tf_op jit(solution)/shard_map/ppermute | solution.py:204
  45.7 1.5 %collective-permute-done.11 = f32[4,320]{1,0:T(4,128)S(1)} collective-permute-done((f32[4,320]{1,0:T(4,128)S(1)}, f32[4,320]{1,0:T(4,128)S(1)}, u32[]{:S(2)}, u32[]{:S(2)}) %collective-permute-start.11) | collective-permute-done | bytes 5152 | tf_op jit(solution)/shard_map/ppermute | solution.py:199
  47.2 0.8 %fusion.11 = f32[4,5,16,256]{3,0,2,1:T(4,128)} fusion(f32[4,5,16,256]{3,0,2,1:T(4,128)S(1)} %bitcast.135, f32[4,5,17,256]{3,0,2,1:T(4,128)S(1)} %multiply_subtract_fusion), kind=kLoop, calls=%fused_computation.21 | loop fusion | flops 245760 | bytes 1310720 | tf_op jit(solution)/shard_map/sub | solution.py:82
  48.2 0.8 %dynamic_update_slice.24 = f32[32,320]{0,1:T(8,128)S(1)} dynamic-update-slice(f32[32,320]{0,1:T(8,128)S(1)} %broadcast_in_dim.21, f32[4,320]{0,1:T(8,128)S(1)} %copy.76, s32[]{:T(128)S(6)} %select_n.188, s32[]{:T(128)} %constant.173.clone.1) | dynamic-update-slice | bytes 10244 | tf_op jit(solution)/shard_map/dynamic_update_slice | solution.py:194
  49.1 1.0 %dynamic_update_slice.25 = f32[32,320]{0,1:T(8,128)S(1)} dynamic-update-slice(f32[32,320]{0,1:T(8,128)S(1)} %dynamic_update_slice.24, f32[4,320]{0,1:T(8,128)S(1)} %copy.77, s32[]{:T(128)S(6)} %select_n.190, s32[]{:T(128)} %constant.173.clone.1) | dynamic-update-slice | bytes 10244 | tf_op jit(solution)/shard_map/dynamic_update_slice | solution.py:200
  50.3 1.0 %dynamic_update_slice.26 = f32[32,320]{0,1:T(8,128)S(1)} dynamic-update-slice(f32[32,320]{0,1:T(8,128)S(1)} %dynamic_update_slice.25, f32[4,320]{0,1:T(8,128)S(1)} %copy.78, s32[]{:T(128)S(6)} %select_n.192, s32[]{:T(128)} %constant.173.clone.1) | dynamic-update-slice | bytes 10244 | tf_op jit(solution)/shard_map/dynamic_update_slice | solution.py:205
  51.5 1.0 %dynamic_update_slice.27 = f32[32,320]{0,1:T(8,128)S(1)} dynamic-update-slice(f32[32,320]{0,1:T(8,128)S(1)} %dynamic_update_slice.26, f32[4,320]{0,1:T(8,128)S(1)} %copy.79, s32[]{:T(128)S(6)} %select_n.194, s32[]{:T(128)} %constant.173.clone.1) | dynamic-update-slice | bytes 10244 | tf_op jit(solution)/shard_map/dynamic_update_slice | solution.py:200
  52.7 1.0 %dynamic_update_slice.28 = f32[32,320]{0,1:T(8,128)S(1)} dynamic-update-slice(f32[32,320]{0,1:T(8,128)S(1)} %dynamic_update_slice.27, f32[4,320]{0,1:T(8,128)S(1)} %copy.80, s32[]{:T(128)S(6)} %select_n.196, s32[]{:T(128)} %constant.173.clone.1) | dynamic-update-slice | bytes 10244 | tf_op jit(solution)/shard_map/dynamic_update_slice | solution.py:205
  53.9 1.0 %dynamic_update_slice.29 = f32[32,320]{0,1:T(8,128)S(1)} dynamic-update-slice(f32[32,320]{0,1:T(8,128)S(1)} %dynamic_update_slice.28, f32[4,320]{0,1:T(8,128)S(1)} %copy.81, s32[]{:T(128)S(6)} %select_n.198, s32[]{:T(128)} %constant.173.clone.1) | dynamic-update-slice | bytes 10244 | tf_op jit(solution)/shard_map/dynamic_update_slice | solution.py:200
  55.1 1.0 %dynamic_update_slice.30 = f32[32,320]{0,1:T(8,128)S(1)} dynamic-update-slice(f32[32,320]{0,1:T(8,128)S(1)} %dynamic_update_slice.29, f32[4,320]{0,1:T(8,128)S(1)} %copy.82, s32[]{:T(128)S(6)} %select_n.200, s32[]{:T(128)} %constant.173.clone.1) | dynamic-update-slice | bytes 10244 | tf_op jit(solution)/shard_map/dynamic_update_slice | solution.py:205
  56.3 1.0 %dynamic_update_slice.31 = f32[32,320]{0,1:T(8,128)S(1)} dynamic-update-slice(f32[32,320]{0,1:T(8,128)S(1)} %dynamic_update_slice.30, f32[4,320]{0,1:T(8,128)S(1)} %copy.83, s32[]{:T(128)S(6)} %select_n.202, s32[]{:T(128)} %constant.173.clone.1) | dynamic-update-slice | bytes 10244 | tf_op jit(solution)/shard_map/dynamic_update_slice | solution.py:200
  57.4 0.4 fusion.27
  57.8 0.6 %broadcast_in_dim.22 = f32[1,5,256]{2,0,1:T(1,128)} reshape(f32[5,256]{1,0:T(8,128)S(1)} %bitcast.149) | data formatting | bytes 10240 | tf_op jit(solution)/shard_map/broadcast_in_dim | solution.py:213
  (104 shorter events, 8.6 us)
Async XLA Ops:
  0.6 1.1 %copy-start = (f32[8,5,4096]{2,0,1:T(8,128)S(1)}, f32[8,5,4096]{2,0,1:T(8,128)}, u32[]{:S(2)}) copy-start(f32[8,5,4096]{2,0,1:T(8,128)} %param.5) | copy-start | bytes 1966084
  0.7 0.7 %copy-start.1 = (s32[32]{0:T(128)S(1)}, s32[32]{0:T(128)}, u32[]{:S(2)}) copy-start(s32[32]{0:T(128)} %param.6) | copy-start | bytes 388
  2.2 7.0 %collective-permute-start.2 = (f32[1,5,4096]{2,1,0:T(8,128)S(1)}, f32[1,5,4096]{2,1,0:T(8,128)S(1)}, u32[]{:S(2)}, u32[]{:S(2)}) collective-permute-start(f32[1,5,4096]{2,1,0:T(8,128)S(1)} %copy.86), channel_id=1, source_target_pairs={{1,0},{2,1},{3,2},{0,3},{5,4},{6,5},{7,6},{4,7},{9,8},{10,9},{11,1... | collective-permute-start | bytes 245768 | tf_op jit(solution)/shard_map/ppermute | solution.py:16
  5.2 6.9 %collective-permute-start.1 = (f32[1,5,4096]{2,1,0:T(8,128)S(1)}, f32[1,5,4096]{2,1,0:T(8,128)S(1)}, u32[]{:S(2)}, u32[]{:S(2)}) collective-permute-start(f32[1,5,4096]{2,1,0:T(8,128)S(1)} %copy.85), channel_id=1, source_target_pairs={{2,0},{3,1},{0,2},{1,3},{6,4},{7,5},{4,6},{5,7},{10,8},{11,9},{8,1... | collective-permute-start | bytes 245768 | tf_op jit(solution)/shard_map/ppermute | solution.py:16
  6.3 6.1 %collective-permute-start = (f32[1,5,4096]{2,1,0:T(8,128)S(1)}, f32[1,5,4096]{2,1,0:T(8,128)S(1)}, u32[]{:S(2)}, u32[]{:S(2)}) collective-permute-start(f32[1,5,4096]{2,1,0:T(8,128)S(1)} %copy.84), channel_id=1, source_target_pairs={{3,0},{0,1},{1,2},{2,3},{7,4},{4,5},{5,6},{6,7},{11,8},{8,9},{9,10... | collective-permute-start | bytes 245768 | tf_op jit(solution)/shard_map/ppermute | solution.py:16
  6.6 0.7 %copy-start.4 = (s32[32]{0:T(128)S(1)}, s32[32]{0:T(128)}, u32[]{:S(2)}) copy-start(s32[32]{0:T(128)} %param.7) | copy-start | bytes 388
  7.8 0.7 %copy-start.2 = (s32[2,16]{1,0:T(2,128)S(1)}, s32[2,16]{1,0:T(2,128)}, u32[]{:S(2)}) copy-start(s32[2,16]{1,0:T(2,128)} %param.8) | copy-start | bytes 388
  8.5 0.7 %copy-start.3 = (s32[1,32]{1,0:T(1,128)S(1)}, s32[1,32]{1,0:T(1,128)}, u32[]{:S(2)}) copy-start(s32[1,32]{1,0:T(1,128)} %param.9) | copy-start | bytes 388
  13.3 9.2 %collective-permute-start.5 = (f32[4,5,2,256]{3,2,1,0:T(2,128)S(1)}, f32[4,5,2,256]{3,2,1,0:T(2,128)S(1)}, u32[]{:S(2)}, u32[]{:S(2)}) collective-permute-start(f32[4,5,2,256]{3,2,1,0:T(2,128)S(1)} %copy.95), channel_id=1, source_target_pairs={{0,1},{1,2},{2,3},{4,5},{5,6},{6,7},{8,9},{9,10},{10,11},{12,13},{... | collective-permute-start | bytes 122888 | tf_op jit(solution)/shard_map/ppermute | solution.py:22
  14.6 8.2 %collective-permute-start.6 = (f32[4,5,2,256]{3,2,1,0:T(2,128)S(1)}, f32[4,5,2,256]{3,2,1,0:T(2,128)S(1)}, u32[]{:S(2)}, u32[]{:S(2)}) collective-permute-start(f32[4,5,2,256]{3,2,1,0:T(2,128)S(1)} %copy.95), channel_id=1, source_target_pairs={{1,0},{2,1},{3,2},{5,4},{6,5},{7,6},{9,8},{10,9},{11,10},{13,12},{... | collective-permute-start | bytes 122888 | tf_op jit(solution)/shard_map/ppermute | solution.py:22
  15.9 7.1 %collective-permute-start.3 = (f32[4,5,2,256]{3,2,1,0:T(2,128)S(1)}, f32[4,5,2,256]{3,2,1,0:T(2,128)S(1)}, u32[]{:S(2)}, u32[]{:S(2)}) collective-permute-start(f32[4,5,2,256]{3,2,1,0:T(2,128)S(1)} %copy.94), channel_id=1, source_target_pairs={{0,1},{1,2},{2,3},{4,5},{5,6},{6,7},{8,9},{9,10},{10,11},{12,13},{... | collective-permute-start | bytes 122888 | tf_op jit(solution)/shard_map/ppermute | solution.py:22
  20.7 4.4 %collective-permute-start.4 = (f32[4,5,2,256]{3,2,1,0:T(2,128)S(1)}, f32[4,5,2,256]{3,2,1,0:T(2,128)S(1)}, u32[]{:S(2)}, u32[]{:S(2)}) collective-permute-start(f32[4,5,2,256]{3,2,1,0:T(2,128)S(1)} %copy.94), channel_id=1, source_target_pairs={{1,0},{2,1},{3,2},{5,4},{6,5},{7,6},{9,8},{10,9},{11,10},{13,12},{... | collective-permute-start | bytes 122888 | tf_op jit(solution)/shard_map/ppermute | solution.py:22
  28.1 6.4 %collective-permute-start.7 = (f32[4,320]{1,0:T(4,128)S(1)}, f32[4,320]{1,0:T(4,128)S(1)}, u32[]{:S(2)}, u32[]{:S(2)}) collective-permute-start(f32[4,320]{1,0:T(4,128)S(1)} %div.74), channel_id=1, source_target_pairs={{0,4},{4,8},{8,12},{12,16},{16,20},{20,24},{24,28},{28,0},{1,5},{5... | collective-permute-start | bytes 15368 | tf_op jit(solution)/shard_map/ppermute | solution.py:199
  29.8 4.8 %collective-permute-start.8 = (f32[4,320]{1,0:T(4,128)S(1)}, f32[4,320]{1,0:T(4,128)S(1)}, u32[]{:S(2)}, u32[]{:S(2)}) collective-permute-start(f32[4,320]{1,0:T(4,128)S(1)} %div.74), channel_id=1, source_target_pairs={{0,28},{4,0},{8,4},{12,8},{16,12},{20,16},{24,20},{28,24},{1,29},{... | collective-permute-start | bytes 15368 | tf_op jit(solution)/shard_map/ppermute | solution.py:204
  34.5 6.3 %collective-permute-start.9 = (f32[4,320]{1,0:T(4,128)S(1)}, f32[4,320]{1,0:T(4,128)S(1)}, u32[]{:S(2)}, u32[]{:S(2)}) collective-permute-start(f32[4,320]{1,0:T(4,128)S(1)} %collective-permute-done.7), channel_id=1, source_target_pairs={{0,4},{4,8},{8,12},{12,16},{16,20},{20,24},{24,28},{28,0},{1,5},{5... | collective-permute-start | bytes 15368 | tf_op jit(solution)/shard_map/ppermute | solution.py:199
  34.6 6.3 %collective-permute-start.10 = (f32[4,320]{1,0:T(4,128)S(1)}, f32[4,320]{1,0:T(4,128)S(1)}, u32[]{:S(2)}, u32[]{:S(2)}) collective-permute-start(f32[4,320]{1,0:T(4,128)S(1)} %collective-permute-done.8), channel_id=1, source_target_pairs={{0,28},{4,0},{8,4},{12,8},{16,12},{20,16},{24,20},{28,24},{1,29},{... | collective-permute-start | bytes 15368 | tf_op jit(solution)/shard_map/ppermute | solution.py:204
  40.9 6.3 %collective-permute-start.11 = (f32[4,320]{1,0:T(4,128)S(1)}, f32[4,320]{1,0:T(4,128)S(1)}, u32[]{:S(2)}, u32[]{:S(2)}) collective-permute-start(f32[4,320]{1,0:T(4,128)S(1)} %collective-permute-done.9), channel_id=1, source_target_pairs={{0,4},{4,8},{8,12},{12,16},{16,20},{20,24},{24,28},{28,0},{1,5},{5... | collective-permute-start | bytes 15368 | tf_op jit(solution)/shard_map/ppermute | solution.py:199
  40.9 14.1 %collective-permute-start.12 = (f32[4,320]{1,0:T(4,128)S(1)}, f32[4,320]{1,0:T(4,128)S(1)}, u32[]{:S(2)}, u32[]{:S(2)}) collective-permute-start(f32[4,320]{1,0:T(4,128)S(1)} %collective-permute-done.10), channel_id=1, source_target_pairs={{0,28},{4,0},{8,4},{12,8},{16,12},{20,16},{24,20},{28,24},{1,29},{... | collective-permute-start | bytes 15368 | tf_op jit(solution)/shard_map/ppermute | solution.py:204
  47.2 8.9 %collective-permute-start.13 = (f32[4,320]{1,0:T(4,128)S(1)}, f32[4,320]{1,0:T(4,128)S(1)}, u32[]{:S(2)}, u32[]{:S(2)}) collective-permute-start(f32[4,320]{1,0:T(4,128)S(1)} %collective-permute-done.11), channel_id=1, source_target_pairs={{0,4},{4,8},{8,12},{12,16},{16,20},{20,24},{24,28},{28,0},{1,5},{5... | collective-permute-start | bytes 15368 | tf_op jit(solution)/shard_map/ppermute | solution.py:199
